TPU v7x, 256 devices: a whole 4x4x8 slice. The times are simulated.
256 devices in a mesh: slab: 4 (over x), row: 64 (over y, z, core).
Axes of the slice: x: 4, y: 4, z: 8, core: 2. Of those that a mesh axis runs over, the one named last changes fastest.
Arguments:
- forcing: bfloat16 [4, 32768, 64], P('slab', 'row'), may hold values from -6 to 6
- inflow: bfloat16 [32768, 64], P('row'), may hold values from -6 to 6
- self_solve: bfloat16 [4, 64, 512, 512], P('slab', 'row'), may hold values from -0.25 to 0.25
- greens: bfloat16 [4, 64, 20, 512, 512], P('slab', 'row'), may hold values from -0.078125 to 0.078125
- kept_cols: int32 [4, 64, 20], P('slab', 'row'), may hold values from 0 to 63, as said below
- counts: int32 [4, 64], P('slab', 'row'), may hold values from 6 to 20, as said below
Outputs:
- traces: bfloat16 [4, 32768, 64], P('slab', 'row')
Inputs may be any that keep to these rules, and one draw needn't show every extreme that they name: `kept_cols`: for each slab and tile row the 20 entries name distinct column tiles. `counts`: in every slab some tile row uses all 20 slots.
All inputs are finite; a program needn't handle non-finite values.
Results may differ from a plain program's by a relative error of at most 0.012.
Values may be sent and summed in bfloat16 or wider, within the bound.
A program may use at most 64 MiB of HBM per device.

v0:
```python
import jax
import jax.numpy as jnp
from jax import lax
from jax.sharding import PartitionSpec as P

TILE = 512


def shifted(array, axis, by):
    size = lax.axis_size(axis)
    pairs = [(i, i + by) for i in range(size) if 0 <= i + by < size]
    return lax.ppermute(array, axis, pairs)


def advance(previous, inflow_cols, forcing_cols, green_row, cols_row, count_row, solve_row):
    arrived = shifted(previous, "slab", 1)
    first_slab = lax.axis_index("slab") == 0
    incoming = jnp.where(first_slab, inflow_cols, arrived)
    gathered = lax.all_gather(incoming, "row", axis=0, tiled=True)
    width = incoming.shape[1]
    tiles = gathered.reshape(-1, TILE, width)
    chosen = tiles[cols_row]
    slot_ids = jnp.arange(green_row.shape[0], dtype=jnp.int32)
    valid = slot_ids < count_row
    chosen = jnp.where(valid[:, None, None], chosen, jnp.zeros((), chosen.dtype))
    total = jnp.einsum("kij,kjw->iw", green_row, chosen, preferred_element_type=jnp.float32)
    coupled = (total + forcing_cols.astype(jnp.float32)).astype(jnp.bfloat16)
    return jnp.dot(solve_row, coupled, preferred_element_type=jnp.float32).astype(jnp.bfloat16)


def shards(forcing, inflow, self_solve, greens, kept_cols, counts):
    slab_count = lax.axis_size("slab")
    green_row = greens[0, 0]
    cols_row = kept_cols[0, 0]
    count_row = counts[0, 0]
    solve_row = self_solve[0, 0]
    source = forcing[0]
    columns = source.shape[1]
    previous = jnp.zeros((TILE, columns), jnp.bfloat16)
    for section in range(slab_count):
        previous = advance(previous, inflow, source, green_row, cols_row, count_row, solve_row)
    return previous[None]


def solution(mesh):
    placed = (
        P("slab", "row", None),
        P("row", None),
        P("slab", "row", None, None),
        P("slab", "row", None, None, None),
        P("slab", "row", None),
        P("slab", "row"),
    )
    return jax.shard_map(
        shards, mesh=mesh, in_specs=placed, out_specs=P("slab", "row", None), check_vma=False
    )
```

profile of v0, /device:TPU:1, one launch (start us, length us, event | category | flops | bytes accessed | tf_op | source)
XLA Modules:
  0.0 408.7 jit_solution(2446877907097513772)
XLA Ops:
  6.5 4.1 collective-permute-start
  10.6 1.3 collective-permute-done
  11.9 1.5 broadcast_select_fusion.3
  13.4 0.0 all-gather.7.cloned.1.call-start
  14.1 0.7 fusion.156
  14.8 79.0 %all-gather.5.cloned.1.call-done = bf16[32768,64]{0,1:T(8,128)(2,1)} async-done(((bf16[512,64]{0,1:T(8,128)(2,1)}), bf16[32768,64]{0,1:T(8,128)(2,1)}) %all-gather.5.cloned.1.call-update) | async-done | bytes 4194320 | tf_op jit(solution)/shard_map/all_gather | solution.py:19
  93.8 4.8 %copy.22 = bf16[8,64,8,512]{3,2,0,1:T(8,128)(2,1)} copy(bf16[8,64,8,512]{3,2,1,0:T(8,128)(2,1)} %bitcast.176) | data formatting | bytes 8388608 | tf_op jit(solution)/shard_map/reshape | solution.py:21
  98.6 2.8 gather_fusion
  101.5 7.5 %fusion.131 = bf16[512,64]{0,1:T(8,128)(2,1)S(1)} fusion(bf16[1,1,20,512,512]{4,3,2,1,0:T(8,128)(2,1)} %param.9, bf16[20,512,64]{1,2,0:T(8,128)(2,1)S(1)} %gather_fusion, pred[20]{0:T(512)(128)(4,1)S(1)} %iota_compare_fusion, bf16[1,1,512,512]{3,2,1,0:T(8,128)(2,1)S(1)} %copy-done, bf16[1,512,64]{1,2,0:T(8,128)(2,1)S(1)} %copy-done.1), kind=kOutput, calls=%fused_computation.47 | convolution fusion | flops 705429504 | bytes 12451860 | tf_op jit(solution)/shard_map/dot_general | solution.py:28
  109.0 3.1 collective-permute-start.1
  112.1 1.3 collective-permute-done.1
  113.4 0.6 broadcast_select_fusion.2
  114.1 0.0 all-gather.9.cloned.1.call-start
  114.2 77.3 %all-gather.7.cloned.1.call-done = bf16[32768,64]{0,1:T(8,128)(2,1)} async-done(((bf16[512,64]{0,1:T(8,128)(2,1)}), bf16[32768,64]{0,1:T(8,128)(2,1)}) %all-gather.7.cloned.1.call-update) | async-done | bytes 4194320 | tf_op jit(solution)/shard_map/all_gather | solution.py:19
  191.4 4.8 %copy.21 = bf16[8,64,8,512]{3,2,0,1:T(8,128)(2,1)} copy(bf16[8,64,8,512]{3,2,1,0:T(8,128)(2,1)} %bitcast.177) | data formatting | bytes 8388608 | tf_op jit(solution)/shard_map/reshape | solution.py:21
  196.2 2.8 gather_fusion.1
  199.1 7.4 %fusion.126 = bf16[512,64]{0,1:T(8,128)(2,1)S(1)} fusion(bf16[1,1,20,512,512]{4,3,2,1,0:T(8,128)(2,1)} %param.9, bf16[20,512,64]{1,2,0:T(8,128)(2,1)S(1)} %gather_fusion.1, pred[20]{0:T(512)(128)(4,1)S(1)} %iota_compare_fusion, bf16[1,1,512,512]{3,2,1,0:T(8,128)(2,1)S(1)} %copy-done, bf16[1,512,64]{1,2,0:T(8,128)(2,1)S(1)} %copy-done.1), kind=kOutput, calls=%fused_computation.46 | convolution fusion | flops 705429504 | bytes 12451860 | tf_op jit(solution)/shard_map/dot_general | solution.py:28
  206.5 3.1 collective-permute-start.2
  209.6 1.3 collective-permute-done.2
  210.9 0.6 broadcast_select_fusion.1
  211.6 0.0 all-gather.11.cloned.1.call-start
  211.6 77.3 %all-gather.9.cloned.1.call-done = bf16[32768,64]{0,1:T(8,128)(2,1)} async-done(((bf16[512,64]{0,1:T(8,128)(2,1)}), bf16[32768,64]{0,1:T(8,128)(2,1)}) %all-gather.9.cloned.1.call-update) | async-done | bytes 4194320 | tf_op jit(solution)/shard_map/all_gather | solution.py:19
  288.9 4.8 %copy.20 = bf16[8,64,8,512]{3,2,0,1:T(8,128)(2,1)} copy(bf16[8,64,8,512]{3,2,1,0:T(8,128)(2,1)} %bitcast.178) | data formatting | bytes 8388608 | tf_op jit(solution)/shard_map/reshape | solution.py:21
  293.7 2.8 gather_fusion.2
  296.6 7.4 %fusion.121 = bf16[512,64]{0,1:T(8,128)(2,1)S(1)} fusion(bf16[1,1,20,512,512]{4,3,2,1,0:T(8,128)(2,1)} %param.9, bf16[20,512,64]{1,2,0:T(8,128)(2,1)S(1)} %gather_fusion.2, pred[20]{0:T(512)(128)(4,1)S(1)} %iota_compare_fusion, bf16[1,1,512,512]{3,2,1,0:T(8,128)(2,1)S(1)} %copy-done, bf16[1,512,64]{1,2,0:T(8,128)(2,1)S(1)} %copy-done.1), kind=kOutput, calls=%fused_computation.45 | convolution fusion | flops 705429504 | bytes 12451860 | tf_op jit(solution)/shard_map/dot_general | solution.py:28
  304.0 3.1 collective-permute-start.3
  307.1 1.3 collective-permute-done.3
  308.4 0.6 broadcast_select_fusion
  309.1 77.3 %all-gather.11.cloned.1.call-done = bf16[32768,64]{0,1:T(8,128)(2,1)} async-done(((bf16[512,64]{0,1:T(8,128)(2,1)}), bf16[32768,64]{0,1:T(8,128)(2,1)}) %all-gather.11.cloned.1.call-update) | async-done | bytes 4194320 | tf_op jit(solution)/shard_map/all_gather | solution.py:19
  386.4 4.8 %copy.19 = bf16[8,64,8,512]{3,2,0,1:T(8,128)(2,1)} copy(bf16[8,64,8,512]{3,2,1,0:T(8,128)(2,1)} %bitcast.179) | data formatting | bytes 8388608 | tf_op jit(solution)/shard_map/reshape | solution.py:21
  391.2 2.8 gather_fusion.3
  394.1 8.1 %fusion.116 = bf16[1,512,64]{1,2,0:T(8,128)(2,1)} fusion(bf16[1,1,20,512,512]{4,3,2,1,0:T(8,128)(2,1)} %param.9, bf16[20,512,64]{1,2,0:T(8,128)(2,1)S(1)} %gather_fusion.3, pred[20]{0:T(512)(128)(4,1)S(1)} %iota_compare_fusion, bf16[1,1,512,512]{3,2,1,0:T(8,128)(2,1)S(1)} %copy-done, bf16[1,512,64]{1,2,0:T(8,128)(2,1)S(1)} %copy-done.1), kind=kOutput, calls=%fused_computation.44 | convolution fusion | flops 705429504 | bytes 12451860 | tf_op jit(solution)/shard_map/dot_general | solution.py:28
  (14 shorter events, 0.1 us)
Async XLA Ops:
  6.5 95.0 %copy-start = (bf16[1,1,512,512]{3,2,1,0:T(8,128)(2,1)S(1)}, bf16[1,1,512,512]{3,2,1,0:T(8,128)(2,1)}, u32[]{:S(2)}) copy-start(bf16[1,1,512,512]{3,2,1,0:T(8,128)(2,1)} %param.8) | copy-start | bytes 1572868
  6.5 87.3 %all-gather.5.cloned.1.call-start = ((), (), s32[]{:S(2)}) async-start(), calls=%async_computation | async-start | bytes 4259840 | tf_op jit(solution)/shard_map/all_gather | solution.py:19
  6.5 5.4 %collective-permute-start = (bf16[512,64]{0,1:T(8,128)(2,1)S(1)}, bf16[512,64]{0,1:T(8,128)(2,1)S(1)}, u32[]{:S(2)}, u32[]{:S(2)}) collective-permute-start(bf16[512,64]{0,1:T(8,128)(2,1)S(1)} %broadcast_in_dim.39), channel_id=1, source_target_pairs={{0,64},{64,128},{128,192},{1,65},{65,129},{129,193},{2,66},{66,130... | collective-permute-start | bytes 196616 | tf_op jit(solution)/shard_map/ppermute | solution.py:12
  13.4 178.0 %all-gather.7.cloned.1.call-start = ((), (), s32[]{:S(2)}) async-start(), calls=%async_computation.1 | async-start | bytes 4259840 | tf_op jit(solution)/shard_map/all_gather | solution.py:19
  98.6 2.9 copy-start.1
  101.5 11.9 %copy-start.2 = (bf16[512,64]{0,1:T(8,128)(2,1)S(1)}, bf16[512,64]{0,1:T(8,128)(2,1)}, u32[]{:S(2)}) copy-start(bf16[512,64]{0,1:T(8,128)(2,1)} %param.7) | copy-start | bytes 196612
  109.0 4.4 %collective-permute-start.1 = (bf16[512,64]{0,1:T(8,128)(2,1)S(1)}, bf16[512,64]{0,1:T(8,128)(2,1)S(1)}, u32[]{:S(2)}, u32[]{:S(2)}) collective-permute-start(bf16[512,64]{0,1:T(8,128)(2,1)S(1)} %fusion.131), channel_id=1, source_target_pairs={{0,64},{64,128},{128,192},{1,65},{65,129},{129,193},{2,66},{66,130... | collective-permute-start | bytes 196616 | tf_op jit(solution)/shard_map/ppermute | solution.py:12
  114.1 174.8 %all-gather.9.cloned.1.call-start = ((), (), s32[]{:S(2)}) async-start(), calls=%async_computation.2 | async-start | bytes 4259840 | tf_op jit(solution)/shard_map/all_gather | solution.py:19
  206.5 4.4 %collective-permute-start.2 = (bf16[512,64]{0,1:T(8,128)(2,1)S(1)}, bf16[512,64]{0,1:T(8,128)(2,1)S(1)}, u32[]{:S(2)}, u32[]{:S(2)}) collective-permute-start(bf16[512,64]{0,1:T(8,128)(2,1)S(1)} %fusion.126), channel_id=1, source_target_pairs={{0,64},{64,128},{128,192},{1,65},{65,129},{129,193},{2,66},{66,130... | collective-permute-start | bytes 196616 | tf_op jit(solution)/shard_map/ppermute | solution.py:12
  211.6 174.8 %all-gather.11.cloned.1.call-start = ((), (), s32[]{:S(2)}) async-start(), calls=%async_computation.3 | async-start | bytes 4259840 | tf_op jit(solution)/shard_map/all_gather | solution.py:19
  304.0 4.4 %collective-permute-start.3 = (bf16[512,64]{0,1:T(8,128)(2,1)S(1)}, bf16[512,64]{0,1:T(8,128)(2,1)S(1)}, u32[]{:S(2)}, u32[]{:S(2)}) collective-permute-start(bf16[512,64]{0,1:T(8,128)(2,1)S(1)} %fusion.121), channel_id=1, source_target_pairs={{0,64},{64,128},{128,192},{1,65},{65,129},{129,193},{2,66},{66,130... | collective-permute-start | bytes 196616 | tf_op jit(solution)/shard_map/ppermute | solution.py:12
Sparse Core Ops, SparseCore 0:
  13.6 80.2 all-gather.4
  114.2 77.1 all-gather.6
  211.7 77.1 all-gather.8
  309.2 77.1 all-gather.10
where the time goes:
time: 409 us
  waiting for transfers between devices  316 us (77%)
  local copies, waits for them, and re-layouts  30.5 us (7%)
  matrix products  30.5 us (7%)
  between operations  13.9 us (3%)
  starting transfers between devices  13.5 us (3%)
    all_gather x4, waiting for transfers between devices, advance(): gathered = lax.all_gather(incoming, 'row', axis=0, tiled=True)  311 us
    dot_general x4, matrix products, advance(): jnp.dot(solve_row, coupled, preferred_element_type=jnp.float32)  30.5 us
    reshape x4, local copies, waits for them, and re-layouts, advance(): tiles = gathered.reshape(-1, TILE, width)  19.2 us
    ppermute x4, starting transfers between devices, shifted(): return lax.ppermute(array, axis, pairs)  13.4 us
    gather x4, local copies, waits for them, and re-layouts, advance(): chosen = tiles[cols_row]  11.3 us
  transfers between devices with their start and end apart: 8, of which 8 were waited for; matrix products, arithmetic and copies ran while one was open for 0% of the time, Pallas kernels for 0%

commit v1 on v0

--- a/solution.py
+++ b/solution.py
@@ -16,7 +16,10 @@
     arrived = shifted(previous, "slab", 1)
     first_slab = lax.axis_index("slab") == 0
     incoming = jnp.where(first_slab, inflow_cols, arrived)
-    gathered = lax.all_gather(incoming, "row", axis=0, tiled=True)
+    count = lax.axis_size("row")
+    blocks = jnp.stack([incoming for _ in range(count)])
+    blocks = lax.all_to_all(blocks, "row", split_axis=0, concat_axis=0)
+    gathered = jnp.concatenate(blocks, axis=0)
     width = incoming.shape[1]
     tiles = gathered.reshape(-1, TILE, width)
     chosen = tiles[cols_row]

time: 409 us -> 485 us (1.19)
  blocking collectives: 0 us -> 308 us
  waiting for transfers between devices: 316 us -> 100 us
  local copies, waits for them, and re-layouts: 30.5 us -> 15.3 us
  starting transfers between devices: 13.5 us -> 28.7 us
  between operations: 13.9 us -> 0.85 us
    all_gather x4 -> x0, waiting for transfers between devices: 311 us -> none  [advance(): gathered = lax.all_gather(incoming, 'row', axis=0, tiled=True)]
    all_to_all x0 -> x3, blocking collectives: none -> 308 us  [advance(): blocks = lax.all_to_all(blocks, 'row', split_axis=0, concat_axis=0)]
    all_to_all x0 -> x1, waiting for transfers between devices: none -> 95.1 us  [advance(): blocks = lax.all_to_all(blocks, 'row', split_axis=0, concat_axis=0)]
    reshape x4 -> x0, local copies, waits for them, and re-layouts: 19.2 us -> none  [advance(): tiles = gathered.reshape(-1, TILE, width)]
    all_to_all x0 -> x1, starting transfers between devices: none -> 13.5 us  [advance(): blocks = lax.all_to_all(blocks, 'row', split_axis=0, concat_axis=0)]
  transfers between devices with their start and end apart: 8 -> 5, of which waited for: 8 -> 5; matrix products, arithmetic and copies ran while one was open for 0% -> 0% of each run, Pallas kernels for 0% -> 0%
where the time goes in v1:
time: 485 us; the launch traced here: 484 us
  blocking collectives  308 us (64%)
  waiting for transfers between devices  100 us (21%)
  matrix products  30.5 us (6%)
  starting transfers between devices  28.7 us (6%)
  local copies, waits for them, and re-layouts  15.3 us (3%)
    all_to_all x3, blocking collectives, advance(): blocks = lax.all_to_all(blocks, 'row', split_axis=0, concat_axis=0)  308 us
    all_to_all x1, waiting for transfers between devices, advance(): blocks = lax.all_to_all(blocks, 'row', split_axis=0, concat_axis=0)  95.1 us
    dot_general x4, matrix products, advance(): jnp.dot(solve_row, coupled, preferred_element_type=jnp.float32)  30.5 us
    ppermute x4, starting transfers between devices, shifted(): return lax.ppermute(array, axis, pairs)  15.2 us
    all_to_all x1, starting transfers between devices, advance(): blocks = lax.all_to_all(blocks, 'row', split_axis=0, concat_axis=0)  13.5 us
    gather x4, local copies, waits for them, and re-layouts, advance(): chosen = tiles[cols_row]  11.3 us
  transfers between devices with their start and end apart: 5, of which 5 were waited for; matrix products, arithmetic and copies ran while one was open for 0% of the time, Pallas kernels for 0%

profile of v1, /device:TPU:1, one launch (start us, length us, event | category | flops | bytes accessed | tf_op | source)
XLA Modules:
  0.0 484.4 jit_solution(18372437495070279112)
XLA Ops:
  0.0 0.0 copy-start
  0.0 4.1 collective-permute-start
  4.1 1.3 collective-permute-done
  5.4 0.8 broadcast_select_fusion.3
  6.2 2.5 stack.8
  8.7 13.5 %all-to-all-start = ((bf16[64,512,64]{1,2,0:T(8,128)(2,1)}), bf16[64,512,64]{1,2,0:T(8,128)(2,1)}, u32[]{:S(2)}, u32[]{:S(2)}) async-start(bf16[64,512,64]{1,2,0:T(8,128)(2,1)} %stack.8), calls=%async_computation | async-start | bytes 8388608 | tf_op jit(solution)/shard_map/all_to_all | solution.py:21
  22.9 0.0 copy-done.3
  22.9 0.0 copy-start.1
  22.9 95.1 %all-to-all-done = bf16[64,512,64]{1,2,0:T(8,128)(2,1)} async-done(((bf16[64,512,64]{1,2,0:T(8,128)(2,1)}), bf16[64,512,64]{1,2,0:T(8,128)(2,1)}, u32[]{:S(2)}, u32[]{:S(2)}) %all-to-all-start) | async-done | bytes 4194336 | tf_op jit(solution)/shard_map/all_to_all | solution.py:21
  118.1 2.8 gather_fusion
  120.9 0.0 copy-done
  120.9 0.0 copy-done.1
  120.9 0.0 copy-start.2
  121.0 7.5 %fusion.131 = bf16[512,64]{0,1:T(8,128)(2,1)S(1)} fusion(bf16[1,1,20,512,512]{4,3,2,1,0:T(8,128)(2,1)} %param.9, bf16[20,512,64]{1,2,0:T(8,128)(2,1)S(1)} %gather_fusion, pred[20]{0:T(512)(128)(4,1)S(1)} %iota_compare_fusion, bf16[1,1,512,512]{3,2,1,0:T(8,128)(2,1)S(1)} %copy-done, bf16[1,512,64]{1,2,0:T(8,128)(2,1)S(1)} %copy-done.1), kind=kOutput, calls=%fused_computation.43 | convolution fusion | flops 705429504 | bytes 12451860 | tf_op jit(solution)/shard_map/dot_general | solution.py:31
  128.4 3.2 collective-permute-start.1
  131.6 1.3 collective-permute-done.1
  132.9 0.5 stack.9
  133.4 102.4 %all_to_all.20 = bf16[64,512,64]{1,2,0:T(8,128)(2,1)} all-to-all(bf16[64,512,64]{1,2,0:T(8,128)(2,1)S(1)} %stack.9), channel_id=1, replica_groups=mesh['slab'=4,'row'=64] {'row'}, dimensions={0} | all-to-all | bytes 8388608 | tf_op jit(solution)/shard_map/all_to_all | solution.py:21
  235.9 2.8 gather_fusion.1
  238.7 7.4 %fusion.126 = bf16[512,64]{0,1:T(8,128)(2,1)S(1)} fusion(bf16[1,1,20,512,512]{4,3,2,1,0:T(8,128)(2,1)} %param.9, bf16[20,512,64]{1,2,0:T(8,128)(2,1)S(1)} %gather_fusion.1, pred[20]{0:T(512)(128)(4,1)S(1)} %iota_compare_fusion, bf16[1,1,512,512]{3,2,1,0:T(8,128)(2,1)S(1)} %copy-done, bf16[1,512,64]{1,2,0:T(8,128)(2,1)S(1)} %copy-done.1), kind=kOutput, calls=%fused_computation.42 | convolution fusion | flops 705429504 | bytes 12451860 | tf_op jit(solution)/shard_map/dot_general | solution.py:31
  246.1 4.0 collective-permute-start.2
  250.1 1.3 collective-permute-done.2
  251.5 0.5 stack.10
  252.0 102.7 %all_to_all.21 = bf16[64,512,64]{1,2,0:T(8,128)(2,1)} all-to-all(bf16[64,512,64]{1,2,0:T(8,128)(2,1)S(1)} %stack.10), channel_id=1, replica_groups=mesh['slab'=4,'row'=64] {'row'}, dimensions={0} | all-to-all | bytes 8388608 | tf_op jit(solution)/shard_map/all_to_all | solution.py:21
  354.7 2.8 gather_fusion.2
  357.5 7.4 %fusion.121 = bf16[512,64]{0,1:T(8,128)(2,1)S(1)} fusion(bf16[1,1,20,512,512]{4,3,2,1,0:T(8,128)(2,1)} %param.9, bf16[20,512,64]{1,2,0:T(8,128)(2,1)S(1)} %gather_fusion.2, pred[20]{0:T(512)(128)(4,1)S(1)} %iota_compare_fusion, bf16[1,1,512,512]{3,2,1,0:T(8,128)(2,1)S(1)} %copy-done, bf16[1,512,64]{1,2,0:T(8,128)(2,1)S(1)} %copy-done.1), kind=kOutput, calls=%fused_computation.41 | convolution fusion | flops 705429504 | bytes 12451860 | tf_op jit(solution)/shard_map/dot_general | solution.py:31
  365.0 4.0 collective-permute-start.3
  369.0 1.3 collective-permute-done.3
  370.3 0.5 stack.11
  370.8 102.7 %all_to_all.22 = bf16[64,512,64]{1,2,0:T(8,128)(2,1)} all-to-all(bf16[64,512,64]{1,2,0:T(8,128)(2,1)S(1)} %stack.11), channel_id=1, replica_groups=mesh['slab'=4,'row'=64] {'row'}, dimensions={0} | all-to-all | bytes 8388608 | tf_op jit(solution)/shard_map/all_to_all | solution.py:21
  473.5 2.8 gather_fusion.3
  476.4 8.1 %fusion.116 = bf16[1,512,64]{1,2,0:T(8,128)(2,1)} fusion(bf16[1,1,20,512,512]{4,3,2,1,0:T(8,128)(2,1)} %param.9, bf16[20,512,64]{1,2,0:T(8,128)(2,1)S(1)} %gather_fusion.3, pred[20]{0:T(512)(128)(4,1)S(1)} %iota_compare_fusion, bf16[1,1,512,512]{3,2,1,0:T(8,128)(2,1)S(1)} %copy-done, bf16[1,512,64]{1,2,0:T(8,128)(2,1)S(1)} %copy-done.1), kind=kOutput, calls=%fused_computation.40 | convolution fusion | flops 705429504 | bytes 12451860 | tf_op jit(solution)/shard_map/dot_general | solution.py:31
  (9 shorter events, 0.1 us)
Async XLA Ops:
  0.0 120.9 %copy-start = (bf16[1,1,512,512]{3,2,1,0:T(8,128)(2,1)S(1)}, bf16[1,1,512,512]{3,2,1,0:T(8,128)(2,1)}, u32[]{:S(2)}) copy-start(bf16[1,1,512,512]{3,2,1,0:T(8,128)(2,1)} %param.8) | copy-start | bytes 1572868
  0.0 5.4 %collective-permute-start = (bf16[512,64]{0,1:T(8,128)(2,1)S(1)}, bf16[512,64]{0,1:T(8,128)(2,1)S(1)}, u32[]{:S(2)}, u32[]{:S(2)}) collective-permute-start(bf16[512,64]{0,1:T(8,128)(2,1)S(1)} %broadcast_in_dim.39), channel_id=1, source_target_pairs={{0,64},{64,128},{128,192},{1,65},{65,129},{129,193},{2,66},{66,130... | collective-permute-start | bytes 196616 | tf_op jit(solution)/shard_map/ppermute | solution.py:12
  8.7 14.2 %copy-start.3 = (s32[1,1,20]{2,1,0:T(1,128)S(1)}, s32[1,1,20]{2,1,0:T(1,128)}, u32[]{:S(2)}) copy-start(s32[1,1,20]{2,1,0:T(1,128)} %param.10) | copy-start | bytes 244
  8.7 109.4 %all-to-all-start = ((bf16[64,512,64]{1,2,0:T(8,128)(2,1)}), bf16[64,512,64]{1,2,0:T(8,128)(2,1)}, u32[]{:S(2)}, u32[]{:S(2)}) async-start(bf16[64,512,64]{1,2,0:T(8,128)(2,1)} %stack.8), calls=%async_computation | async-start | bytes 8388608 | tf_op jit(solution)/shard_map/all_to_all | solution.py:21
  22.9 98.0 %copy-start.1 = (bf16[1,512,64]{1,2,0:T(8,128)(2,1)S(1)}, bf16[1,512,64]{1,2,0:T(8,128)(2,1)}, u32[]{:S(2)}) copy-start(bf16[1,512,64]{1,2,0:T(8,128)(2,1)} %param.6) | copy-start | bytes 196612
  120.9 12.0 %copy-start.2 = (bf16[512,64]{0,1:T(8,128)(2,1)S(1)}, bf16[512,64]{0,1:T(8,128)(2,1)}, u32[]{:S(2)}) copy-start(bf16[512,64]{0,1:T(8,128)(2,1)} %param.7) | copy-start | bytes 196612
  128.4 4.5 collective-permute-start.1
  246.1 5.3 %collective-permute-start.2 = (bf16[512,64]{0,1:T(8,128)(2,1)S(1)}, bf16[512,64]{0,1:T(8,128)(2,1)S(1)}, u32[]{:S(2)}, u32[]{:S(2)}) collective-permute-start(bf16[512,64]{0,1:T(8,128)(2,1)S(1)} %fusion.126), channel_id=1, source_target_pairs={{0,64},{64,128},{128,192},{1,65},{65,129},{129,193},{2,66},{66,130... | collective-permute-start | bytes 196616 | tf_op jit(solution)/shard_map/ppermute | solution.py:12
  365.0 5.3 %collective-permute-start.3 = (bf16[512,64]{0,1:T(8,128)(2,1)S(1)}, bf16[512,64]{0,1:T(8,128)(2,1)S(1)}, u32[]{:S(2)}, u32[]{:S(2)}) collective-permute-start(bf16[512,64]{0,1:T(8,128)(2,1)S(1)} %fusion.121), channel_id=1, source_target_pairs={{0,64},{64,128},{128,192},{1,65},{65,129},{129,193},{2,66},{66,130... | collective-permute-start | bytes 196616 | tf_op jit(solution)/shard_map/ppermute | solution.py:12
